TPU v7x, 128 devices: a whole 4x4x4 slice. The times are simulated.
128 devices in a mesh: slab: 16 (over z, x), pencil: 8 (over y, core).
Axes of the slice: x: 4, y: 4, z: 4, core: 2. Of those that a mesh axis runs over, the one named last changes fastest.
Arguments:
- a_blocks: float32 [256, 64, 20480], P('slab', 'pencil'), may hold values from -1 to 8, as said below
- col_codes: int32 [256, 64, 5], P('slab', 'pencil'), may hold values from 0 to 8, as said below
- agg_of: int32 [256, 64], P('slab', 'pencil'), may hold values from 0 to 2047, as said below
- test_vectors: float32 [256, 64, 2048], P('slab', 'pencil'), may hold values from -36 to 36
Outputs:
- relaxed: float32 [256, 64, 2048], P('slab', 'pencil')
- tiles: float32 [256, 64, 512], P('slab', 'pencil')
- products: float32 [256, 64, 2560], P('slab', 'pencil')
Inputs may be any that keep to these rules, and one draw needn't show every extreme that they name: `col_codes`: slot 0 of every block row is code 4, the block row itself; slots 1 to 4 hold different codes among the other eight of the 3 x 3 neighbourhood. `agg_of`: aggregate g is owned by device g // 16, devices numbered slab-major. On each device the block rows, in row-major order, form 64 groups of 2 consecutive block rows; all block rows of a group belong to aggregates of one owner, and the groups of one device go to different owners. Some owners receive a group from every device. `a_blocks`: the diagonal entries of every slot-0 block lie in [1.99, 8].
All inputs are finite; a program needn't handle non-finite values.
Results may differ from a plain program's by a relative error of at most 0.0003.
Values sent between devices are 32-bit elements; how exact they have to be, the bound alone decides.
A program may use at most 320 MiB of HBM per device.

v0:
```python
import math
import jax
import jax.numpy as jnp
from jax import lax
from jax.sharding import PartitionSpec as P

BLK = 64
NV = 32
NC = 8
KS = 5
ITERS = 2
OMEGA = 2.0 / 3.0
FULL_PRECISION = lax.Precision.HIGHEST


def with_halo(cells, sides, width):
    for axis, dim in sides:
        count = lax.axis_size(axis)
        ends = count - 1
        head = lax.slice_in_dim(cells, 0, width, axis=dim)
        tail = lax.slice_in_dim(cells, cells.shape[dim] - width, cells.shape[dim], axis=dim)
        cells = jnp.concatenate(
            [
                lax.ppermute(tail, axis, [(i, (i + 1) % count) for i in range(ends)]),
                cells,
                lax.ppermute(head, axis, [((i + 1) % count, i) for i in range(ends)]),
            ],
            axis=dim,
        )
    return cells


def coarse_modes(cells, coarse):
    centre = jnp.arange(cells, dtype=jnp.float32) + 0.5
    order = jnp.arange(coarse, dtype=jnp.float32)
    return jnp.cos(math.pi * centre[:, None] * order[None, :] / cells)


def solve_maps(coarse):
    gram = jnp.einsum("gkv,glv->gkl", coarse, coarse, precision=FULL_PRECISION)
    trace_sum = jnp.trace(gram, axis1=1, axis2=2)
    ridge = 0.1 * trace_sum / NC + 1e-06
    gram = gram + ridge[:, None, None] * jnp.eye(NC, dtype=jnp.float32)[None]
    lower = jnp.linalg.cholesky(gram)
    half_solved = jax.scipy.linalg.solve_triangular(lower, coarse, lower=True)
    solved = jax.scipy.linalg.solve_triangular(lower, half_solved, lower=True, trans=1)
    return jnp.swapaxes(solved, 1, 2)


def slot_index(col_codes):
    height, across_devices = (col_codes.shape[0], col_codes.shape[1])
    row_pos = jnp.arange(height, dtype=jnp.int32)[:, None, None] + col_codes // 3
    col_pos = jnp.arange(across_devices, dtype=jnp.int32)[None, :, None] + col_codes % 3
    return (row_pos * (across_devices + 2) + col_pos).reshape(-1)


def pick_rows(padded, flat_index, height, across_devices):
    features = padded.shape[2]
    flat = padded.reshape(padded.shape[0] * padded.shape[1], features)
    picked = jnp.take(flat, flat_index, axis=0)
    return picked.reshape(height, across_devices, KS, features)


def fit_slots(slot_coefficient, slot_ids, per_owner):
    members = (slot_ids[None, :] == jnp.arange(per_owner, dtype=jnp.int32)[:, None]).astype(
        jnp.float32
    )
    counts = jnp.sum(members, axis=1)
    summed = jnp.dot(
        members,
        slot_coefficient.reshape(slot_coefficient.shape[0], NC * NV),
        precision=FULL_PRECISION,
    )
    coarse = summed.reshape(per_owner, NC, NV) / jnp.maximum(counts, 1.0)[:, None, None]
    maps = solve_maps(coarse)
    return jnp.dot(members.T, maps.reshape(per_owner, NV * NC), precision=FULL_PRECISION)


def pack_slots(chosen_f, payload, group_list, capacity):
    flat = payload.reshape(group_list, capacity * payload.shape[1])
    packed = jnp.dot(chosen_f, flat, precision=FULL_PRECISION)
    return packed.reshape(chosen_f.shape[0], capacity, payload.shape[1])


def unpack_slots(chosen_f, received, block_rows):
    flat = received.reshape(received.shape[0], received.shape[1] * received.shape[2])
    return jnp.dot(chosen_f.T, flat, precision=FULL_PRECISION).reshape(
        block_rows, received.shape[2]
    )


def send_owner(payload, slot_ids):
    arrived, arrived_ids = (
        lax.all_to_all(payload, ("slab", "pencil"), split_axis=0, concat_axis=0, tiled=True),
        lax.all_to_all(slot_ids, ("slab", "pencil"), split_axis=0, concat_axis=0, tiled=True),
    )
    return (arrived, arrived_ids)


def send_back(payload):
    returned = lax.all_to_all(payload, ("slab", "pencil"), split_axis=0, concat_axis=0, tiled=True)
    return returned


def shards(a_blocks, col_codes, agg_of, test_vectors):
    height, across_devices = (agg_of.shape[0], agg_of.shape[1])
    n_slab = lax.axis_size("slab")
    n_pencil = lax.axis_size("pencil")
    devices = n_slab * n_pencil
    blocks = a_blocks.reshape(height, across_devices, KS, BLK, BLK)
    diagonal = jnp.diagonal(blocks[:, :, 0], axis1=-2, axis2=-1)
    block_wide = jnp.transpose(blocks, (0, 1, 3, 2, 4)).reshape(
        height, across_devices, BLK, KS * BLK
    )
    flat_index = slot_index(col_codes)
    candidate_vectors = test_vectors.reshape(height, across_devices, BLK, NV)
    for sweep in range(ITERS):
        padded = with_halo(
            candidate_vectors.reshape(height, across_devices, BLK * NV),
            (("slab", 0), ("pencil", 1)),
            1,
        )
        picked = pick_rows(padded, flat_index, height, across_devices).reshape(
            height, across_devices, KS * BLK, NV
        )
        image = jnp.einsum("ijor,ijrw->ijow", block_wide, picked, precision=FULL_PRECISION)
        candidate_vectors = candidate_vectors - OMEGA * image / diagonal[:, :, :, None]
    squares = jnp.sum(candidate_vectors * candidate_vectors, axis=(0, 1, 2))
    totals = lax.psum(squares, ("slab", "pencil"))
    scale = jnp.sqrt(totals / (height * across_devices * BLK * devices) + 1e-06)
    relaxed = candidate_vectors / scale
    block_rows = height * across_devices
    capacity = 2 * block_rows // devices
    group_list = devices // 2
    per_owner = block_rows // 8
    near_null_modes = coarse_modes(BLK, NC)
    row_vectors = relaxed.reshape(block_rows, BLK, NV)
    group_agg = agg_of.reshape(group_list, capacity)
    group_owner = group_agg[:, 0] // per_owner
    chosen = group_owner[None, :] == jnp.arange(devices, dtype=jnp.int32)[:, None]
    chosen_f = chosen.astype(jnp.float32)
    slot_ids = (
        jnp.sum(jnp.where(chosen[:, :, None], group_agg[None] % per_owner + 1, 0), axis=1) - 1
    )
    slot_count = devices * capacity
    outgoing = pack_slots(chosen_f, row_vectors.reshape(block_rows, BLK * NV), group_list, capacity)
    arrived, arrived_ids = send_owner(outgoing, slot_ids)
    slot_vector_rows = arrived.reshape(slot_count, BLK, NV)
    slot_coefficient = jnp.einsum(
        "wd,xwf->xdf", near_null_modes, slot_vector_rows, precision=FULL_PRECISION
    )
    slot_maps = fit_slots(slot_coefficient, arrived_ids.reshape(slot_count), per_owner)
    slot_tiles = jnp.einsum(
        "scv,svk->sck",
        slot_vector_rows,
        slot_maps.reshape(slot_count, NV, NC),
        precision=FULL_PRECISION,
    )
    returned = send_back(slot_tiles.reshape(devices, capacity, BLK * NC))
    tile_rows = unpack_slots(chosen_f, returned, block_rows).reshape(block_rows, BLK, NC)
    tile_grid = tile_rows.reshape(height, across_devices, BLK * NC)
    padded_tiles = with_halo(tile_grid, (("slab", 0), ("pencil", 1)), 1)
    picked_tiles = pick_rows(padded_tiles, flat_index, height, across_devices).reshape(
        height, across_devices, KS, BLK, NC
    )
    products = jnp.einsum("ijkoc,ijkcw->ijkow", blocks, picked_tiles, precision=FULL_PRECISION)
    return (
        relaxed.reshape(height, across_devices, BLK * NV),
        tile_grid,
        products.reshape(height, across_devices, KS * BLK * NC),
    )


def solution(mesh):
    in_specs = (
        P("slab", "pencil", None),
        P("slab", "pencil", None),
        P("slab", "pencil"),
        P("slab", "pencil", None),
    )
    out_specs = (P("slab", "pencil", None), P("slab", "pencil", None), P("slab", "pencil", None))
    return jax.shard_map(shards, mesh=mesh, in_specs=in_specs, out_specs=out_specs, check_vma=False)
```

profile of v0, /device:TPU:7, one launch (start us, length us, event | category | flops | bytes accessed | tf_op | source)
XLA Modules:
  0.0 639.7 jit_solution(15918062208513373529)
XLA Ops:
  4.1 4.9 collective-permute-start
  11.9 38.9 %copy.177 = f32[16,8,20480]{0,1,2:T(8,128)} copy(f32[16,8,20480]{2,1,0:T(8,128)} %param.6) | data formatting | bytes 20971520 | tf_op args[0]
  50.9 11.6 %slice_bitcast_fusion = f32[16,8,64,64]{0,1,3,2:T(8,128)} fusion(f32[16,8,5,64,64]{0,1,4,3,2:T(8,128)} %bitcast), kind=kLoop, calls=%fused_computation.6 | loop fusion | bytes 4194304 | tf_op jit(solution)/shard_map/squeeze | solution.py:111
  76.0 6.4 %gather_fusion = f32[64,16,8]{1,2,0:T(8,128)S(1)} fusion(f32[16,8,64,64]{0,1,3,2:T(8,128)} %slice_bitcast_fusion, s32[64]{0:T(128)S(1)} %or_bitcast_fusion), kind=kCustom, calls=%fused_computation.2 | custom fusion | bytes 66048 | tf_op jit(solution)/shard_map/jit(diagonal)/gather | solution.py:111
  82.6 63.1 %copy.178 = f32[16,8,64,5,64]{2,4,3,1,0:T(8,128)} copy(f32[16,8,64,5,64]{0,1,4,2,3:T(8,128)} %bitcast.1) | data formatting | bytes 20971520 | tf_op jit(solution)/shard_map/transpose | solution.py:112
  150.0 4.6 gather_fusion.2
  154.6 5.2 broadcast_select_fusion.1
  159.8 13.7 %reshape_reshape.7 = f32[16,8,320,32]{3,2,1,0:T(8,128)} reshape(f32[640,2048]{1,0:T(8,128)} %broadcast_select_fusion.1) | data formatting | bytes 10485760 | tf_op jit(solution)/shard_map/reshape;reshape | solution.py:123
  173.5 37.9 %bitcast_subtract_fusion.1 = f32[16,8,64,32]{2,3,1,0:T(8,128)S(1)} fusion(f32[16,8,64,32]{2,3,1,0:T(8,128)} %copy.182, f32[16,8,320,32]{3,2,1,0:T(8,128)} %reshape_reshape.7, f32[16,8,64,320]{2,3,1,0:T(8,128)} %bitcast.82, f32[16,8,64]{2,1,0:T(8,128)S(1)} %copy.181), kind=kOutput, calls=%fused_computation.13 | convolution fusion | flops 1007419392 | bytes 17858560 | tf_op jit(solution)/shard_map/ijor,ijrw->ijow/dot_general | solution.py:126
  224.2 4.7 collective-permute-start.6
  231.6 10.5 %all-to-all-start.1 = ((s32[128,1,2]{2,1,0:T(1,128)}), s32[128,1,2]{2,1,0:T(1,128)S(1)}, u32[]{:S(2)}, u32[]{:S(2)}) async-start(s32[128,1,2]{2,1,0:T(1,128)} %copy.196), calls=%async_computation.1 | async-start | bytes 131072 | tf_op jit(solution)/shard_map/all_to_all | solution.py:95
  245.7 4.6 gather_fusion.3
  250.2 5.2 broadcast_select_fusion
  255.5 13.8 %reshape_reshape.8 = f32[16,8,320,32]{3,2,1,0:T(8,128)} reshape(f32[640,2048]{1,0:T(8,128)} %broadcast_select_fusion) | data formatting | bytes 10485760 | tf_op jit(solution)/shard_map/reshape;reshape | solution.py:123
  269.3 38.3 %multiply_reduce_fusion = (f32[32]{0:T(128)S(1)}, f32[16,8,64,32]{2,3,1,0:T(8,128)}) fusion(f32[16,8,64,32]{2,3,1,0:T(8,128)S(1)} %copy-done.1, f32[16,8,64]{2,1,0:T(8,128)S(1)} %copy.181, f32[16,8,320,32]{3,2,1,0:T(8,128)} %reshape_reshape.8, f32[16,8,64,320]{2,3,1,0:T(8,128)} %bitcast.83), kind=kOutput, calls=%fused_computation.14 | convolution fusion | flops 1007943680 | bytes 17858688 | tf_op jit(solution)/shard_map/ijor,ijrw->ijow/dot_general | solution.py:126
  307.6 65.2 %psum.7 = f32[32]{0:T(128)S(1)} all-reduce(f32[32]{0:T(128)S(1)} %get-tuple-element.33), channel_id=1, replica_groups=mesh['slab'=16,'pencil'=8] {'slab','pencil'}, use_global_device_ids=true, to_apply=%region_1.3 | all-reduce | flops 32 | bytes 256 | tf_op jit(solution)/shard_map/psum | solution.py:129
  385.2 7.3 %all-to-all-start = ((f32[128,2,2048]{2,1,0:T(2,128)}), f32[128,2,2048]{2,1,0:T(2,128)S(1)}, u32[]{:S(2)}, u32[]{:S(2)}) async-start(f32[128,2,2048]{2,1,0:T(2,128)} %copy.192), calls=%async_computation | async-start | bytes 4194304 | tf_op jit(solution)/shard_map/all_to_all | solution.py:94
  394.1 26.8 %all-to-all-done = f32[128,2,2048]{2,1,0:T(2,128)S(1)} async-done(((f32[128,2,2048]{2,1,0:T(2,128)}), f32[128,2,2048]{2,1,0:T(2,128)S(1)}, u32[]{:S(2)}, u32[]{:S(2)}) %all-to-all-start) | async-done | bytes 2097184 | tf_op jit(solution)/shard_map/all_to_all | solution.py:94
  421.0 5.3 reshape.246
  426.3 7.0 %copy.197 = f32[256,64,32]{0,1,2:T(8,128)S(1)} copy(f32[256,64,32]{2,1,0:T(8,128)} %reshape.246) | data formatting | bytes 4194304 | tf_op jit(solution)/shard_map/reshape | solution.py:148
  435.6 11.7 %custom-call.11 = f32[16,8,8]{2,1,0:T(8,128)S(1)} custom-call(f32[16,8,8]{2,1,0:T(8,128)S(1)} %fusion.18), custom_call_target="Cholesky" | custom-call | tf_op jit(solution)/shard_map/jit(cholesky)/cholesky | solution.py:44
  447.6 10.0 %custom-call.12 = f32[16,1,8,8]{2,3,1,0:T(8,128)S(1)} custom-call(f32[16,1,8,8]{3,2,1,0:T(8,128)S(1)} %select_bitcast_fusion), custom_call_target="InvertDiagBlocksLowerTriangular" | custom-call | tf_op jit(solution)/shard_map/jit(_solve_triangular)/vmap()/triangular_solve | solution.py:46
  459.0 11.2 %fusion.56 = f32[256,64,8]{2,1,0:T(8,128)} fusion(f32[256,64,32]{2,1,0:T(8,128)} %reshape.246, f32[256,32,8]{1,2,0:T(8,128)S(1)} %copy.209), kind=kOutput, calls=%fused_computation.114 | convolution fusion | flops 50331648 | bytes 2883584 | tf_op jit(solution)/shard_map/scv,svk->sck/dot_general | solution.py:153
  470.2 7.4 %reshape.249 = f32[128,2,512]{2,1,0:T(2,128)} reshape(f32[256,64,8]{2,1,0:T(8,128)} %fusion.56) | data formatting | bytes 1048576 | tf_op jit(solution)/shard_map/reshape | solution.py:159
  477.6 6.3 all-to-all-start.2
  484.1 11.8 %all-to-all-done.2 = f32[128,2,512]{2,1,0:T(2,128)S(1)} async-done(((f32[128,2,512]{2,1,0:T(2,128)}), f32[128,2,512]{2,1,0:T(2,128)S(1)}, u32[]{:S(2)}, u32[]{:S(2)}) %all-to-all-start.2) | async-done | bytes 524320 | tf_op jit(solution)/shard_map/all_to_all | solution.py:101
  502.2 4.6 collective-permute-done.9
  512.7 55.6 %copy.214 = f32[16,8,5,64,64]{4,3,2,1,0:T(8,128)} copy(f32[16,8,5,64,64]{0,1,4,3,2:T(8,128)} %bitcast) | data formatting | bytes 20971520 | tf_op jit(solution)/shard_map/reshape | solution.py:110
  575.2 13.6 %gather.15 = f32[16,8,5,64,8]{4,3,2,1,0:T(8,128)} reshape(f32[640,512]{1,0:T(8,128)S(1)} %gather_fusion.1) | data formatting | bytes 2621440 | tf_op jit(solution)/shard_map/jit(_take)/gather | solution.py:60
  588.8 37.9 %fusion.4 = f32[16,8,5,64,8]{3,4,2,1,0:T(8,128)S(1)} fusion(f32[16,8,5,64,64]{4,3,2,1,0:T(8,128)} %copy.214, f32[16,8,5,64,8]{4,3,2,1,0:T(8,128)} %gather.15, pred[16,8,5]{2,1,0:T(8,128)(4,1)S(1)} %copy.211), kind=kOutput, calls=%fused_computation.16 | convolution fusion | flops 251985920 | bytes 13107840 | tf_op jit(solution)/shard_map/ijkoc,ijkcw->ijkow/dot_general | solution.py:166
  626.7 6.0 copy.215
  632.7 6.8 %copy.216 = f32[16,8,2560]{2,1,0:T(8,128)} copy(f32[16,8,2560]{0,2,1:T(8,128)} %bitcast.84) | data formatting | bytes 2621440
  (128 shorter events, 80.2 us)
Async XLA Ops:
  1.6 61.6 %collective-permute-start.1 = (f32[1,8,2048]{2,0,1:T(1,128)S(1)}, f32[1,8,2048]{2,0,1:T(1,128)S(1)}, u32[]{:S(2)}, u32[]{:S(2)}) collective-permute-start(f32[1,8,2048]{2,0,1:T(1,128)S(1)} %copy.174), channel_id=1, source_target_pairs={{8,0},{16,8},{24,16},{32,24},{40,32},{48,40},{56,48},{64,56},{72,6... | collective-permute-start | bytes 196616 | tf_op jit(solution)/shard_map/ppermute | solution.py:26
  4.1 59.0 %collective-permute-start = (f32[1,8,2048]{2,0,1:T(1,128)S(1)}, f32[1,8,2048]{2,0,1:T(1,128)S(1)}, u32[]{:S(2)}, u32[]{:S(2)}) collective-permute-start(f32[1,8,2048]{2,0,1:T(1,128)S(1)} %copy.173), channel_id=1, source_target_pairs={{0,8},{8,16},{16,24},{24,32},{32,40},{40,48},{48,56},{56,64},{64,7... | collective-permute-start | bytes 196616 | tf_op jit(solution)/shard_map/ppermute | solution.py:24
  11.6 39.3 %copy-start.4 = (s32[16,8,5]{2,1,0:T(8,128)}, s32[16,8,5]{2,1,0:T(8,128)S(1)}, u32[]{:S(2)}) copy-start(s32[16,8,5]{2,1,0:T(8,128)S(1)} %copy.172) | copy-start | bytes 7684
  11.9 39.0 %copy-start.7 = (s32[64]{0:T(128)}, s32[64]{0:T(128)S(1)}, u32[]{:S(2)}) copy-start(s32[64]{0:T(128)S(1)} %and_select_fusion.1) | copy-start | bytes 772
  50.9 11.7 %copy-start.2 = (f32[16,8,2048]{2,1,0:T(8,128)S(1)}, f32[16,8,2048]{2,1,0:T(8,128)}, u32[]{:S(2)}) copy-start(f32[16,8,2048]{2,1,0:T(8,128)} %param.9) | copy-start | bytes 3145732
  63.2 82.5 %collective-permute-start.2 = (f32[18,1,2048]{2,0,1:T(8,128)S(1)}, f32[18,1,2048]{2,0,1:T(8,128)S(1)}, u32[]{:S(2)}, u32[]{:S(2)}) collective-permute-start(f32[18,1,2048]{2,0,1:T(8,128)S(1)} %get-tuple-element.25), channel_id=1, source_target_pairs={{0,1},{1,2},{2,3},{3,4},{4,5},{5,6},{6,7},{8,9},{9,10},{10,11},{11... | collective-permute-start | bytes 442376 | tf_op jit(solution)/shard_map/ppermute | solution.py:24
  67.6 78.2 %collective-permute-start.3 = (f32[18,1,2048]{2,0,1:T(8,128)S(1)}, f32[18,1,2048]{2,0,1:T(8,128)S(1)}, u32[]{:S(2)}, u32[]{:S(2)}) collective-permute-start(f32[18,1,2048]{2,0,1:T(8,128)S(1)} %get-tuple-element.26), channel_id=1, source_target_pairs={{1,0},{2,1},{3,2},{4,3},{5,4},{6,5},{7,6},{9,8},{10,9},{11,10},{12... | collective-permute-start | bytes 442376 | tf_op jit(solution)/shard_map/ppermute | solution.py:26
  211.4 5.2 copy-start
  211.7 12.2 %collective-permute-start.4 = (f32[1,8,2048]{2,1,0:T(8,128)S(1)}, f32[1,8,2048]{2,1,0:T(8,128)S(1)}, u32[]{:S(2)}, u32[]{:S(2)}) collective-permute-start(f32[1,8,2048]{2,1,0:T(8,128)S(1)} %slice.78), channel_id=1, source_target_pairs={{0,8},{8,16},{16,24},{24,32},{32,40},{40,48},{48,56},{56,64},{64,7... | collective-permute-start | bytes 196616 | tf_op jit(solution)/shard_map/ppermute | solution.py:24
  216.8 7.1 %collective-permute-start.5 = (f32[1,8,2048]{2,1,0:T(8,128)S(1)}, f32[1,8,2048]{2,1,0:T(8,128)S(1)}, u32[]{:S(2)}, u32[]{:S(2)}) collective-permute-start(f32[1,8,2048]{2,1,0:T(8,128)S(1)} %slice.80), channel_id=1, source_target_pairs={{8,0},{16,8},{24,16},{32,24},{40,32},{48,40},{56,48},{64,56},{72,6... | collective-permute-start | bytes 196616 | tf_op jit(solution)/shard_map/ppermute | solution.py:26
  224.2 18.0 %collective-permute-start.6 = (f32[18,1,2048]{2,1,0:T(1,128)S(1)}, f32[18,1,2048]{2,1,0:T(1,128)S(1)}, u32[]{:S(2)}, u32[]{:S(2)}) collective-permute-start(f32[18,1,2048]{2,1,0:T(1,128)S(1)} %get-tuple-element.23), channel_id=1, source_target_pairs={{0,1},{1,2},{2,3},{3,4},{4,5},{5,6},{6,7},{8,9},{9,10},{10,11},{11... | collective-permute-start | bytes 442376 | tf_op jit(solution)/shard_map/ppermute | solution.py:24
  228.9 13.2 %collective-permute-start.7 = (f32[18,1,2048]{2,1,0:T(1,128)S(1)}, f32[18,1,2048]{2,1,0:T(1,128)S(1)}, u32[]{:S(2)}, u32[]{:S(2)}) collective-permute-start(f32[18,1,2048]{2,1,0:T(1,128)S(1)} %get-tuple-element.24), channel_id=1, source_target_pairs={{1,0},{2,1},{3,2},{4,3},{5,4},{6,5},{7,6},{9,8},{10,9},{11,10},{12... | collective-permute-start | bytes 442376 | tf_op jit(solution)/shard_map/ppermute | solution.py:26
  231.6 153.6 %all-to-all-start.1 = ((s32[128,1,2]{2,1,0:T(1,128)}), s32[128,1,2]{2,1,0:T(1,128)S(1)}, u32[]{:S(2)}, u32[]{:S(2)}) async-start(s32[128,1,2]{2,1,0:T(1,128)} %copy.196), calls=%async_computation.1 | async-start | bytes 131072 | tf_op jit(solution)/shard_map/all_to_all | solution.py:95
  255.5 13.8 %copy-start.1 = (f32[16,8,64,32]{2,3,1,0:T(8,128)S(1)}, f32[16,8,64,32]{2,3,1,0:T(8,128)}, u32[]{:S(2)}) copy-start(f32[16,8,64,32]{2,3,1,0:T(8,128)} %copy-done) | copy-start | bytes 3145732
  377.6 3.5 copy-start.8
  385.2 35.8 %all-to-all-start = ((f32[128,2,2048]{2,1,0:T(2,128)}), f32[128,2,2048]{2,1,0:T(2,128)S(1)}, u32[]{:S(2)}, u32[]{:S(2)}) async-start(f32[128,2,2048]{2,1,0:T(2,128)} %copy.192), calls=%async_computation | async-start | bytes 4194304 | tf_op jit(solution)/shard_map/all_to_all | solution.py:94
  470.2 13.7 %copy-start.5 = (s32[16,8,5]{2,1,0:T(8,128)S(1)}, s32[16,8,5]{2,1,0:T(8,128)}, u32[]{:S(2)}) copy-start(s32[16,8,5]{2,1,0:T(8,128)} %copy-done.4) | copy-start | bytes 7684
  477.6 18.3 %all-to-all-start.2 = ((f32[128,2,512]{2,1,0:T(2,128)}), f32[128,2,512]{2,1,0:T(2,128)S(1)}, u32[]{:S(2)}, u32[]{:S(2)}) async-start(f32[128,2,512]{2,1,0:T(2,128)} %reshape.249), calls=%async_computation.2 | async-start | bytes 1048576 | tf_op jit(solution)/shard_map/all_to_all | solution.py:101
  496.3 5.8 collective-permute-start.8
  500.1 68.1 %copy-start.3 = (f32[16,8,512]{2,1,0:T(8,128)}, f32[16,8,512]{2,1,0:T(8,128)S(1)}, u32[]{:S(2)}) copy-start(f32[16,8,512]{2,1,0:T(8,128)S(1)} %reshape_reshape_reshape.7) | copy-start | bytes 786436
  500.2 6.6 %collective-permute-start.9 = (f32[1,8,512]{2,1,0:T(8,128)S(1)}, f32[1,8,512]{2,1,0:T(8,128)S(1)}, u32[]{:S(2)}, u32[]{:S(2)}) collective-permute-start(f32[1,8,512]{2,1,0:T(8,128)S(1)} %slice.87), channel_id=1, source_target_pairs={{8,0},{16,8},{24,16},{32,24},{40,32},{48,40},{56,48},{64,56},{72,6... | collective-permute-start | bytes 49160 | tf_op jit(solution)/shard_map/ppermute | solution.py:26
  506.8 66.1 %collective-permute-start.10 = (f32[18,1,512]{2,1,0:T(1,128)S(1)}, f32[18,1,512]{2,1,0:T(1,128)S(1)}, u32[]{:S(2)}, u32[]{:S(2)}) collective-permute-start(f32[18,1,512]{2,1,0:T(1,128)S(1)} %get-tuple-element.29), channel_id=1, source_target_pairs={{0,1},{1,2},{2,3},{3,4},{4,5},{5,6},{6,7},{8,9},{9,10},{10,11},{11... | collective-permute-start | bytes 110600 | tf_op jit(solution)/shard_map/ppermute | solution.py:24
  509.9 63.0 %collective-permute-start.11 = (f32[18,1,512]{2,1,0:T(1,128)S(1)}, f32[18,1,512]{2,1,0:T(1,128)S(1)}, u32[]{:S(2)}, u32[]{:S(2)}) collective-permute-start(f32[18,1,512]{2,1,0:T(1,128)S(1)} %get-tuple-element.30), channel_id=1, source_target_pairs={{1,0},{2,1},{3,2},{4,3},{5,4},{6,5},{7,6},{9,8},{10,9},{11,10},{12... | collective-permute-start | bytes 110600 | tf_op jit(solution)/shard_map/ppermute | solution.py:26
  512.7 55.6 %copy-start.6 = (pred[16,8,5]{0,1,2:T(8,128)(4,1)S(1)}, pred[16,8,5]{0,1,2:T(8,128)(4,1)}, u32[]{:S(2)}) copy-start(pred[16,8,5]{0,1,2:T(8,128)(4,1)} %get-tuple-element.19) | copy-start | bytes 1924
where the time goes:
time: 651 us; the launch traced here: 640 us
  local copies, waits for them, and re-layouts  300 us (46%)
  matrix products  130 us (20%)
  blocking collectives  65.2 us (10%)
  starting transfers between devices  61.2 us (9%)
  waiting for transfers between devices  43.2 us (7%)
  other arithmetic  39.2 us (6%)
    dot_general x2, matrix products, shards(): jnp.einsum('ijor,ijrw->ijow', block_wide, picked, precision=FULL_PRECISION)  76.2 us
    psum x1, blocking collectives, shards(): totals = lax.psum(squares, ('slab', 'pencil'))  65.2 us
    transpose x1, local copies, waits for them, and re-layouts, shards(): jnp.transpose(blocks, (0, 1, 3, 2, 4))  63.1 us
    reshape x1, local copies, waits for them, and re-layouts, shards(): blocks = a_blocks.reshape(height, across_devices, KS, BLK, BLK)  55.6 us
    unnamed x27, local copies, waits for them, and re-layouts  47.3 us
    dot_general x1, matrix products, shards(): jnp.einsum('ijkoc,ijkcw->ijkow', blocks, picked_tiles, precision=FULL_PRE...  37.9 us
    another operation x2, local copies, waits for them, and re-layouts, shards(): pick_rows(padded, flat_index, height, across_devices)  27.5 us
    all_to_all x1, waiting for transfers between devices, send_owner(): lax.all_to_all(payload, ('slab', 'pencil'), split_axis=0, concat_axis=0,...  26.8 us
  transfers between devices with their start and end apart: 15, of which 3 were waited for; matrix products, arithmetic and copies ran while one was open for 43% of the time, Pallas kernels for 0%

commit v1 on v0

--- a/solution.py
+++ b/solution.py
@@ -126,7 +126,8 @@
         image = jnp.einsum("ijor,ijrw->ijow", block_wide, picked, precision=FULL_PRECISION)
         candidate_vectors = candidate_vectors - OMEGA * image / diagonal[:, :, :, None]
     squares = jnp.sum(candidate_vectors * candidate_vectors, axis=(0, 1, 2))
-    totals = lax.psum(squares, ("slab", "pencil"))
+    parts = lax.all_gather(squares, ("slab", "pencil"))
+    totals = jnp.sum(parts, axis=0)
     scale = jnp.sqrt(totals / (height * across_devices * BLK * devices) + 1e-06)
     relaxed = candidate_vectors / scale
     block_rows = height * across_devices

time: 651 us -> 651 us (level)
    psum x1 -> x0, blocking collectives: 65.2 us -> none  [shards(): totals = lax.psum(squares, ('slab', 'pencil'))]
    unnamed x0 -> x1, blocking collectives: none -> 65.2 us
    unnamed x27 -> x29, local copies, waits for them, and re-layouts: 47.3 us -> 47.6 us
where the time goes in v1:
time: 651 us; the launch traced here: 640 us
  local copies, waits for them, and re-layouts  300 us (46%)
  matrix products  130 us (20%)
  blocking collectives  65.2 us (10%)
  starting transfers between devices  61.1 us (9%)
  waiting for transfers between devices  43.2 us (7%)
  other arithmetic  39.3 us (6%)
    dot_general x2, matrix products, shards(): jnp.einsum('ijor,ijrw->ijow', block_wide, picked, precision=FULL_PRECISION)  76.2 us
    unnamed x1, blocking collectives  65.2 us
    transpose x1, local copies, waits for them, and re-layouts, shards(): jnp.transpose(blocks, (0, 1, 3, 2, 4))  63.1 us
    reshape x1, local copies, waits for them, and re-layouts, shards(): blocks = a_blocks.reshape(height, across_devices, KS, BLK, BLK)  55.6 us
    unnamed x29, local copies, waits for them, and re-layouts  47.6 us
    dot_general x1, matrix products, shards(): jnp.einsum('ijkoc,ijkcw->ijkow', blocks, picked_tiles, precision=FULL_PRE...  37.9 us
    another operation x2, local copies, waits for them, and re-layouts, shards(): pick_rows(padded, flat_index, height, across_devices)  27.5 us
    all_to_all x1, waiting for transfers between devices, send_owner(): lax.all_to_all(payload, ('slab', 'pencil'), split_axis=0, concat_axis=0,...  26.8 us
  transfers between devices with their start and end apart: 15, of which 3 were waited for; matrix products, arithmetic and copies ran while one was open for 43% of the time, Pallas kernels for 0%

profile of v1, /device:TPU:7, one launch (start us, length us, event | category | flops | bytes accessed | tf_op | source)
XLA Modules:
  0.0 640.1 jit_solution(8501627585861475378)
XLA Ops:
  4.1 4.9 collective-permute-start
  11.9 38.9 %copy.177 = f32[16,8,20480]{0,1,2:T(8,128)} copy(f32[16,8,20480]{2,1,0:T(8,128)} %param.6) | data formatting | bytes 20971520 | tf_op args[0]
  50.9 11.6 %slice_bitcast_fusion = f32[16,8,64,64]{0,1,3,2:T(8,128)} fusion(f32[16,8,5,64,64]{0,1,4,3,2:T(8,128)} %bitcast), kind=kLoop, calls=%fused_computation.6 | loop fusion | bytes 4194304 | tf_op jit(solution)/shard_map/squeeze | solution.py:111
  76.0 6.4 %gather_fusion = f32[64,16,8]{1,2,0:T(8,128)S(1)} fusion(f32[16,8,64,64]{0,1,3,2:T(8,128)} %slice_bitcast_fusion, s32[64]{0:T(128)S(1)} %or_bitcast_fusion), kind=kCustom, calls=%fused_computation.2 | custom fusion | bytes 66048 | tf_op jit(solution)/shard_map/jit(diagonal)/gather | solution.py:111
  82.6 63.1 %copy.178 = f32[16,8,64,5,64]{2,4,3,1,0:T(8,128)} copy(f32[16,8,64,5,64]{0,1,4,2,3:T(8,128)} %bitcast.1) | data formatting | bytes 20971520 | tf_op jit(solution)/shard_map/transpose | solution.py:112
  150.0 4.6 gather_fusion.2
  154.6 5.2 broadcast_select_fusion.1
  159.8 13.7 %reshape_reshape.7 = f32[16,8,320,32]{3,2,1,0:T(8,128)} reshape(f32[640,2048]{1,0:T(8,128)} %broadcast_select_fusion.1) | data formatting | bytes 10485760 | tf_op jit(solution)/shard_map/reshape;reshape | solution.py:123
  173.5 37.9 %bitcast_subtract_fusion.1 = f32[16,8,64,32]{2,3,1,0:T(8,128)S(1)} fusion(f32[16,8,64,32]{2,3,1,0:T(8,128)} %copy.182, f32[16,8,320,32]{3,2,1,0:T(8,128)} %reshape_reshape.7, f32[16,8,64,320]{2,3,1,0:T(8,128)} %bitcast.82, f32[16,8,64]{2,1,0:T(8,128)S(1)} %copy.181), kind=kOutput, calls=%fused_computation.13 | convolution fusion | flops 1007419392 | bytes 17858560 | tf_op jit(solution)/shard_map/ijor,ijrw->ijow/dot_general | solution.py:126
  224.2 4.7 collective-permute-start.6
  231.6 10.5 %all-to-all-start.1 = ((s32[128,1,2]{2,1,0:T(1,128)}), s32[128,1,2]{2,1,0:T(1,128)S(1)}, u32[]{:S(2)}, u32[]{:S(2)}) async-start(s32[128,1,2]{2,1,0:T(1,128)} %copy.196), calls=%async_computation.1 | async-start | bytes 131072 | tf_op jit(solution)/shard_map/all_to_all | solution.py:95
  245.7 4.6 gather_fusion.3
  250.2 5.2 broadcast_select_fusion
  255.4 13.8 %reshape_reshape.8 = f32[16,8,320,32]{3,2,1,0:T(8,128)} reshape(f32[640,2048]{1,0:T(8,128)} %broadcast_select_fusion) | data formatting | bytes 10485760 | tf_op jit(solution)/shard_map/reshape;reshape | solution.py:123
  269.3 38.3 %multiply_reduce_fusion = (f32[32]{0:T(128)S(1)}, f32[16,8,64,32]{2,3,1,0:T(8,128)}) fusion(f32[16,8,64,32]{2,3,1,0:T(8,128)S(1)} %copy-done.1, f32[16,8,64]{2,1,0:T(8,128)S(1)} %copy.181, f32[16,8,320,32]{3,2,1,0:T(8,128)} %reshape_reshape.8, f32[16,8,64,320]{2,3,1,0:T(8,128)} %bitcast.83), kind=kOutput, calls=%fused_computation.14 | convolution fusion | flops 1007943680 | bytes 17858688 | tf_op jit(solution)/shard_map/ijor,ijrw->ijow/dot_general | solution.py:126
  307.9 65.2 %all-reduce = f32[4096]{0:T(1024)S(1)} all-reduce(f32[4096]{0:T(1024)S(1)} %dynamic-update-slice.3), channel_id=2, replica_groups=mesh['slab'=16,'pencil'=8] {'slab','pencil'}, use_global_device_ids=true, to_apply=%add | all-reduce | flops 4096 | bytes 32768
  385.6 7.2 %all-to-all-start = ((f32[128,2,2048]{2,1,0:T(2,128)}), f32[128,2,2048]{2,1,0:T(2,128)S(1)}, u32[]{:S(2)}, u32[]{:S(2)}) async-start(f32[128,2,2048]{2,1,0:T(2,128)} %copy.192), calls=%async_computation | async-start | bytes 4194304 | tf_op jit(solution)/shard_map/all_to_all | solution.py:94
  394.5 26.8 %all-to-all-done = f32[128,2,2048]{2,1,0:T(2,128)S(1)} async-done(((f32[128,2,2048]{2,1,0:T(2,128)}), f32[128,2,2048]{2,1,0:T(2,128)S(1)}, u32[]{:S(2)}, u32[]{:S(2)}) %all-to-all-start) | async-done | bytes 2097184 | tf_op jit(solution)/shard_map/all_to_all | solution.py:94
  421.3 5.3 reshape.250
  426.6 7.0 %copy.197 = f32[256,64,32]{0,1,2:T(8,128)S(1)} copy(f32[256,64,32]{2,1,0:T(8,128)} %reshape.250) | data formatting | bytes 4194304 | tf_op jit(solution)/shard_map/reshape | solution.py:149
  435.9 11.7 %custom-call.11 = f32[16,8,8]{2,1,0:T(8,128)S(1)} custom-call(f32[16,8,8]{2,1,0:T(8,128)S(1)} %fusion.18), custom_call_target="Cholesky" | custom-call | tf_op jit(solution)/shard_map/jit(cholesky)/cholesky | solution.py:44
  447.9 10.0 %custom-call.12 = f32[16,1,8,8]{2,3,1,0:T(8,128)S(1)} custom-call(f32[16,1,8,8]{3,2,1,0:T(8,128)S(1)} %select_bitcast_fusion), custom_call_target="InvertDiagBlocksLowerTriangular" | custom-call | tf_op jit(solution)/shard_map/jit(_solve_triangular)/vmap()/triangular_solve | solution.py:46
  459.3 11.2 %fusion.56 = f32[256,64,8]{2,1,0:T(8,128)} fusion(f32[256,64,32]{2,1,0:T(8,128)} %reshape.250, f32[256,32,8]{1,2,0:T(8,128)S(1)} %copy.209), kind=kOutput, calls=%fused_computation.114 | convolution fusion | flops 50331648 | bytes 2883584 | tf_op jit(solution)/shard_map/scv,svk->sck/dot_general | solution.py:154
  470.5 7.4 %reshape.253 = f32[128,2,512]{2,1,0:T(2,128)} reshape(f32[256,64,8]{2,1,0:T(8,128)} %fusion.56) | data formatting | bytes 1048576 | tf_op jit(solution)/shard_map/reshape | solution.py:160
  477.8 6.3 all-to-all-start.2
  484.4 11.8 %all-to-all-done.2 = f32[128,2,512]{2,1,0:T(2,128)S(1)} async-done(((f32[128,2,512]{2,1,0:T(2,128)}), f32[128,2,512]{2,1,0:T(2,128)S(1)}, u32[]{:S(2)}, u32[]{:S(2)}) %all-to-all-start.2) | async-done | bytes 524320 | tf_op jit(solution)/shard_map/all_to_all | solution.py:101
  502.5 4.6 collective-permute-done.9
  513.0 55.6 %copy.214 = f32[16,8,5,64,64]{4,3,2,1,0:T(8,128)} copy(f32[16,8,5,64,64]{0,1,4,3,2:T(8,128)} %bitcast) | data formatting | bytes 20971520 | tf_op jit(solution)/shard_map/reshape | solution.py:110
  575.6 13.5 %gather.15 = f32[16,8,5,64,8]{4,3,2,1,0:T(8,128)} reshape(f32[640,512]{1,0:T(8,128)S(1)} %gather_fusion.1) | data formatting | bytes 2621440 | tf_op jit(solution)/shard_map/jit(_take)/gather | solution.py:60
  589.1 37.9 %fusion.4 = f32[16,8,5,64,8]{3,4,2,1,0:T(8,128)S(1)} fusion(f32[16,8,5,64,64]{4,3,2,1,0:T(8,128)} %copy.214, f32[16,8,5,64,8]{4,3,2,1,0:T(8,128)} %gather.15, pred[16,8,5]{2,1,0:T(8,128)(4,1)S(1)} %copy.211), kind=kOutput, calls=%fused_computation.16 | convolution fusion | flops 251985920 | bytes 13107840 | tf_op jit(solution)/shard_map/ijkoc,ijkcw->ijkow/dot_general | solution.py:167
  627.0 6.1 copy.215
  633.1 6.8 %copy.216 = f32[16,8,2560]{2,1,0:T(8,128)} copy(f32[16,8,2560]{0,2,1:T(8,128)} %bitcast.84) | data formatting | bytes 2621440
  (132 shorter events, 80.6 us)
Async XLA Ops:
  1.6 61.6 %collective-permute-start.1 = (f32[1,8,2048]{2,0,1:T(1,128)S(1)}, f32[1,8,2048]{2,0,1:T(1,128)S(1)}, u32[]{:S(2)}, u32[]{:S(2)}) collective-permute-start(f32[1,8,2048]{2,0,1:T(1,128)S(1)} %copy.174), channel_id=1, source_target_pairs={{8,0},{16,8},{24,16},{32,24},{40,32},{48,40},{56,48},{64,56},{72,6... | collective-permute-start | bytes 196616 | tf_op jit(solution)/shard_map/ppermute | solution.py:26
  4.1 59.0 %collective-permute-start = (f32[1,8,2048]{2,0,1:T(1,128)S(1)}, f32[1,8,2048]{2,0,1:T(1,128)S(1)}, u32[]{:S(2)}, u32[]{:S(2)}) collective-permute-start(f32[1,8,2048]{2,0,1:T(1,128)S(1)} %copy.173), channel_id=1, source_target_pairs={{0,8},{8,16},{16,24},{24,32},{32,40},{40,48},{48,56},{56,64},{64,7... | collective-permute-start | bytes 196616 | tf_op jit(solution)/shard_map/ppermute | solution.py:24
  11.6 39.3 %copy-start.4 = (s32[16,8,5]{2,1,0:T(8,128)}, s32[16,8,5]{2,1,0:T(8,128)S(1)}, u32[]{:S(2)}) copy-start(s32[16,8,5]{2,1,0:T(8,128)S(1)} %copy.172) | copy-start | bytes 7684
  11.9 39.0 %copy-start.7 = (s32[64]{0:T(128)}, s32[64]{0:T(128)S(1)}, u32[]{:S(2)}) copy-start(s32[64]{0:T(128)S(1)} %and_select_fusion.1) | copy-start | bytes 772
  50.9 11.7 %copy-start.2 = (f32[16,8,2048]{2,1,0:T(8,128)S(1)}, f32[16,8,2048]{2,1,0:T(8,128)}, u32[]{:S(2)}) copy-start(f32[16,8,2048]{2,1,0:T(8,128)} %param.9) | copy-start | bytes 3145732
  63.2 82.5 %collective-permute-start.2 = (f32[18,1,2048]{2,0,1:T(8,128)S(1)}, f32[18,1,2048]{2,0,1:T(8,128)S(1)}, u32[]{:S(2)}, u32[]{:S(2)}) collective-permute-start(f32[18,1,2048]{2,0,1:T(8,128)S(1)} %get-tuple-element.25), channel_id=1, source_target_pairs={{0,1},{1,2},{2,3},{3,4},{4,5},{5,6},{6,7},{8,9},{9,10},{10,11},{11... | collective-permute-start | bytes 442376 | tf_op jit(solution)/shard_map/ppermute | solution.py:24
  67.6 78.2 %collective-permute-start.3 = (f32[18,1,2048]{2,0,1:T(8,128)S(1)}, f32[18,1,2048]{2,0,1:T(8,128)S(1)}, u32[]{:S(2)}, u32[]{:S(2)}) collective-permute-start(f32[18,1,2048]{2,0,1:T(8,128)S(1)} %get-tuple-element.26), channel_id=1, source_target_pairs={{1,0},{2,1},{3,2},{4,3},{5,4},{6,5},{7,6},{9,8},{10,9},{11,10},{12... | collective-permute-start | bytes 442376 | tf_op jit(solution)/shard_map/ppermute | solution.py:26
  211.4 5.2 copy-start
  211.7 12.2 %collective-permute-start.4 = (f32[1,8,2048]{2,1,0:T(8,128)S(1)}, f32[1,8,2048]{2,1,0:T(8,128)S(1)}, u32[]{:S(2)}, u32[]{:S(2)}) collective-permute-start(f32[1,8,2048]{2,1,0:T(8,128)S(1)} %slice.78), channel_id=1, source_target_pairs={{0,8},{8,16},{16,24},{24,32},{32,40},{40,48},{48,56},{56,64},{64,7... | collective-permute-start | bytes 196616 | tf_op jit(solution)/shard_map/ppermute | solution.py:24
  216.8 7.1 %collective-permute-start.5 = (f32[1,8,2048]{2,1,0:T(8,128)S(1)}, f32[1,8,2048]{2,1,0:T(8,128)S(1)}, u32[]{:S(2)}, u32[]{:S(2)}) collective-permute-start(f32[1,8,2048]{2,1,0:T(8,128)S(1)} %slice.80), channel_id=1, source_target_pairs={{8,0},{16,8},{24,16},{32,24},{40,32},{48,40},{56,48},{64,56},{72,6... | collective-permute-start | bytes 196616 | tf_op jit(solution)/shard_map/ppermute | solution.py:26
  224.2 18.0 %collective-permute-start.6 = (f32[18,1,2048]{2,1,0:T(1,128)S(1)}, f32[18,1,2048]{2,1,0:T(1,128)S(1)}, u32[]{:S(2)}, u32[]{:S(2)}) collective-permute-start(f32[18,1,2048]{2,1,0:T(1,128)S(1)} %get-tuple-element.23), channel_id=1, source_target_pairs={{0,1},{1,2},{2,3},{3,4},{4,5},{5,6},{6,7},{8,9},{9,10},{10,11},{11... | collective-permute-start | bytes 442376 | tf_op jit(solution)/shard_map/ppermute | solution.py:24
  228.9 13.2 %collective-permute-start.7 = (f32[18,1,2048]{2,1,0:T(1,128)S(1)}, f32[18,1,2048]{2,1,0:T(1,128)S(1)}, u32[]{:S(2)}, u32[]{:S(2)}) collective-permute-start(f32[18,1,2048]{2,1,0:T(1,128)S(1)} %get-tuple-element.24), channel_id=1, source_target_pairs={{1,0},{2,1},{3,2},{4,3},{5,4},{6,5},{7,6},{9,8},{10,9},{11,10},{12... | collective-permute-start | bytes 442376 | tf_op jit(solution)/shard_map/ppermute | solution.py:26
  231.6 154.0 %all-to-all-start.1 = ((s32[128,1,2]{2,1,0:T(1,128)}), s32[128,1,2]{2,1,0:T(1,128)S(1)}, u32[]{:S(2)}, u32[]{:S(2)}) async-start(s32[128,1,2]{2,1,0:T(1,128)} %copy.196), calls=%async_computation.1 | async-start | bytes 131072 | tf_op jit(solution)/shard_map/all_to_all | solution.py:95
  255.4 13.8 %copy-start.1 = (f32[16,8,64,32]{2,3,1,0:T(8,128)S(1)}, f32[16,8,64,32]{2,3,1,0:T(8,128)}, u32[]{:S(2)}) copy-start(f32[16,8,64,32]{2,3,1,0:T(8,128)} %copy-done) | copy-start | bytes 3145732
  378.0 3.5 copy-start.8
  385.6 35.7 %all-to-all-start = ((f32[128,2,2048]{2,1,0:T(2,128)}), f32[128,2,2048]{2,1,0:T(2,128)S(1)}, u32[]{:S(2)}, u32[]{:S(2)}) async-start(f32[128,2,2048]{2,1,0:T(2,128)} %copy.192), calls=%async_computation | async-start | bytes 4194304 | tf_op jit(solution)/shard_map/all_to_all | solution.py:94
  470.5 13.7 %copy-start.5 = (s32[16,8,5]{2,1,0:T(8,128)S(1)}, s32[16,8,5]{2,1,0:T(8,128)}, u32[]{:S(2)}) copy-start(s32[16,8,5]{2,1,0:T(8,128)} %copy-done.4) | copy-start | bytes 7684
  477.8 18.3 %all-to-all-start.2 = ((f32[128,2,512]{2,1,0:T(2,128)}), f32[128,2,512]{2,1,0:T(2,128)S(1)}, u32[]{:S(2)}, u32[]{:S(2)}) async-start(f32[128,2,512]{2,1,0:T(2,128)} %reshape.253), calls=%async_computation.2 | async-start | bytes 1048576 | tf_op jit(solution)/shard_map/all_to_all | solution.py:101
  496.6 5.8 collective-permute-start.8
  500.4 68.2 %copy-start.3 = (f32[16,8,512]{2,1,0:T(8,128)}, f32[16,8,512]{2,1,0:T(8,128)S(1)}, u32[]{:S(2)}) copy-start(f32[16,8,512]{2,1,0:T(8,128)S(1)} %reshape_reshape_reshape.7) | copy-start | bytes 786436
  500.5 6.6 %collective-permute-start.9 = (f32[1,8,512]{2,1,0:T(8,128)S(1)}, f32[1,8,512]{2,1,0:T(8,128)S(1)}, u32[]{:S(2)}, u32[]{:S(2)}) collective-permute-start(f32[1,8,512]{2,1,0:T(8,128)S(1)} %slice.87), channel_id=1, source_target_pairs={{8,0},{16,8},{24,16},{32,24},{40,32},{48,40},{56,48},{64,56},{72,6... | collective-permute-start | bytes 49160 | tf_op jit(solution)/shard_map/ppermute | solution.py:26
  507.1 66.1 %collective-permute-start.10 = (f32[18,1,512]{2,1,0:T(1,128)S(1)}, f32[18,1,512]{2,1,0:T(1,128)S(1)}, u32[]{:S(2)}, u32[]{:S(2)}) collective-permute-start(f32[18,1,512]{2,1,0:T(1,128)S(1)} %get-tuple-element.29), channel_id=1, source_target_pairs={{0,1},{1,2},{2,3},{3,4},{4,5},{5,6},{6,7},{8,9},{9,10},{10,11},{11... | collective-permute-start | bytes 110600 | tf_op jit(solution)/shard_map/ppermute | solution.py:24
  510.2 63.0 %collective-permute-start.11 = (f32[18,1,512]{2,1,0:T(1,128)S(1)}, f32[18,1,512]{2,1,0:T(1,128)S(1)}, u32[]{:S(2)}, u32[]{:S(2)}) collective-permute-start(f32[18,1,512]{2,1,0:T(1,128)S(1)} %get-tuple-element.30), channel_id=1, source_target_pairs={{1,0},{2,1},{3,2},{4,3},{5,4},{6,5},{7,6},{9,8},{10,9},{11,10},{12... | collective-permute-start | bytes 110600 | tf_op jit(solution)/shard_map/ppermute | solution.py:26
  513.0 55.6 %copy-start.6 = (pred[16,8,5]{0,1,2:T(8,128)(4,1)S(1)}, pred[16,8,5]{0,1,2:T(8,128)(4,1)}, u32[]{:S(2)}) copy-start(pred[16,8,5]{0,1,2:T(8,128)(4,1)} %get-tuple-element.19) | copy-start | bytes 1924
